TPU v7x, 512 devices: a whole 4x8x8 slice. The times are simulated.
512 devices in a mesh: tm: 64 (over z, x, core), band: 8 (over y).
Axes of the slice: x: 4, y: 8, z: 8, core: 2. Of those that a mesh axis runs over, the one named last changes fastest.
Arguments:
- query_input: bfloat16 [64, 40, 26, 1120], P('tm', 'band'), may hold values from -6 to 6
- key_input: bfloat16 [64, 40, 26, 1120], P('tm', 'band'), may hold values from -8 to 8
- value_input: bfloat16 [64, 40, 26, 1120], P('tm', 'band'), may hold values from -12 to 12
- cotangent: bfloat16 [64, 40, 26, 1120], P('tm', 'band'), may hold values from -6 to 6
- local_kernel_weight: float32 [3, 3, 1120], replicated, may hold values from -2 to 2
Outputs:
- mixed_out: bfloat16 [64, 40, 26, 1120], P('tm', 'band')
- query_grad: bfloat16 [64, 40, 26, 1120], P('tm', 'band')
- key_grad: bfloat16 [64, 40, 26, 1120], P('tm', 'band')
- value_grad: bfloat16 [64, 40, 26, 1120], P('tm', 'band')
- kernel_grad: float32 [3, 3, 1120], replicated
All inputs are finite; a program needn't handle non-finite values.
Results may differ from a plain program's by a relative error of at most 0.018.
Values may be sent and summed in bfloat16 or wider, within the bound.
No kernel may reach another device: no remote copies, remote signals or barrier semaphores. Data moves between devices by JAX's collectives and lax.ppermute only.
A program may use at most 128 MiB of HBM per device.

v0:
```python
import math
import jax
import jax.numpy as jnp
from jax import lax
from jax.sharding import PartitionSpec as P

HEADS = 35
HEAD_DIM = 32


def entering(shard, axis, combine, identity, reverse):
    devices, mine = (lax.axis_size(axis), lax.axis_index(axis))
    everything = jax.tree.map(lambda part: lax.all_gather(part, axis), shard)
    start = jax.tree.map(
        lambda part, zero: jnp.broadcast_to(jnp.asarray(zero, part.dtype), part.shape),
        shard,
        identity,
    )

    def step(k, before):
        at = devices - 1 - k if reverse else k
        reached = at > mine if reverse else at < mine
        new = combine(before, jax.tree.map(lambda part: part[at], everything))
        return jax.tree.map(lambda a, b: jnp.where(reached, a, b), new, before)

    return lax.fori_loop(0, devices, step, start)


def padded(cells, sides, width):
    for axis, dim in sides:
        count = lax.axis_size(axis)
        ends = count - 1
        head = lax.slice_in_dim(cells, 0, width, axis=dim)
        tail = lax.slice_in_dim(cells, cells.shape[dim] - width, cells.shape[dim], axis=dim)
        cells = jnp.concatenate(
            [
                lax.ppermute(tail, axis, [(i, (i + 1) % count) for i in range(ends)]),
                cells,
                lax.ppermute(head, axis, [((i + 1) % count, i) for i in range(ends)]),
            ],
            axis=dim,
        )
    return cells


def feature(x):
    return jnp.where(x > 0, x + 1.0, jnp.exp(jnp.minimum(x, 0.0)))


def slope(x):
    return jnp.where(x > 0, jnp.ones_like(x), jnp.exp(jnp.minimum(x, 0.0)))


def add_pair(earlier, later_term):
    return (earlier[0] + later_term[0], earlier[1] + later_term[1])


def frame_totals(terms, backward):
    frame = lax.psum(terms, "band")
    start = (jnp.zeros_like(frame[0]), jnp.zeros_like(frame[1]))
    before = entering(frame, "tm", add_pair, start, backward)
    return add_pair(before, frame)


def group_heads_count():
    chosen = 1
    for candidate in range(1, HEADS + 1):
        if HEADS % candidate == 0 and candidate * HEAD_DIM <= 256:
            chosen = candidate
    return chosen


def block_outer(left, right, group_count, group_heads, precise):
    count = left.shape[0]
    group_width = group_heads * HEAD_DIM
    left_groups = left.reshape(count, group_count, group_width)
    right_groups = right.reshape(count, group_count, group_width)
    if precise:
        whole = jnp.einsum(
            "tga,tgb->gab", left_groups, right_groups, precision=lax.Precision.HIGHEST
        )
    else:
        whole = jnp.einsum(
            "tga,tgb->gab", left_groups, right_groups, preferred_element_type=jnp.float32
        )
    whole = whole.reshape(group_count, group_heads, HEAD_DIM, group_heads, HEAD_DIM)
    same_head = jnp.eye(group_heads, dtype=jnp.float32)[None, :, None, :, None]
    return jnp.sum(whole * same_head, axis=3).reshape(HEADS, HEAD_DIM, HEAD_DIM)


def block_matrix(state, group_count, group_heads):
    group_width = group_heads * HEAD_DIM
    placed = state.reshape(group_count, group_heads, HEAD_DIM, 1, HEAD_DIM)
    same_head = jnp.eye(group_heads, dtype=jnp.float32)[None, :, None, :, None]
    return (placed * same_head).reshape(group_count, group_width, group_width)


def apply_blocks(rows, blocks, transposed):
    count = rows.shape[0]
    group_count, group_width = (blocks.shape[0], blocks.shape[1])
    grouped = rows.reshape(count, group_count, group_width)
    if transposed:
        result = jnp.einsum("tgb,gab->tga", grouped, blocks, precision=lax.Precision.HIGHEST)
    else:
        result = jnp.einsum("tga,gab->tgb", grouped, blocks, precision=lax.Precision.HIGHEST)
    return result.reshape(count, group_count * group_width)


def shards(query_input, key_input, value_input, cotangent, local_kernel_weight):
    high = lax.Precision.HIGHEST
    band_row_span, column_count, width = (
        query_input.shape[1],
        query_input.shape[2],
        query_input.shape[3],
    )
    count = band_row_span * column_count
    group_heads = group_heads_count()
    group_count = HEADS // group_heads
    indicator = (jnp.arange(width)[:, None] // HEAD_DIM == jnp.arange(HEADS)[None, :]).astype(
        jnp.float32
    )
    q_raw = query_input[0].reshape(count, width).astype(jnp.float32)
    k_raw = key_input[0].reshape(count, width).astype(jnp.float32)
    q_feat = feature(q_raw).astype(jnp.bfloat16)
    k_feat = feature(k_raw).astype(jnp.bfloat16)
    value_flat = value_input[0].reshape(count, width)
    own_state = block_outer(k_feat, value_flat, group_count, group_heads, False)
    own_norm = jnp.sum(k_feat, axis=0, dtype=jnp.float32).reshape(HEADS, HEAD_DIM)
    state, norm_vec = frame_totals((own_state, own_norm), False)
    q_wide = q_feat.astype(jnp.float32)
    state_blocks = block_matrix(state, group_count, group_heads)
    norm_flat = norm_vec.reshape(width)
    num = apply_blocks(q_wide, state_blocks, False)
    den = jnp.dot(q_wide * norm_flat, indicator, precision=high)
    den_wide = jnp.dot(den, indicator.T, precision=high)
    attn = num / den_wide
    stacked = jnp.stack([value_input[0], cotangent[0]])
    rimmed = padded(stacked, (("band", 1),), 1)
    padded_input = jnp.pad(rimmed, ((0, 0), (0, 0), (1, 1), (0, 0)))
    value_padded = padded_input[0]
    gpad = padded_input[1]
    complete_gradient = cotangent[0].astype(jnp.float32)
    local_output = jnp.zeros((band_row_span, column_count, width), jnp.float32)
    v_local = jnp.zeros((band_row_span, column_count, width), jnp.float32)
    kernel_row_slice = []
    for row_offset in range(3):
        for column_offset in range(3):
            local_output = (
                local_output
                + local_kernel_weight[row_offset, column_offset]
                * value_padded[
                    row_offset : row_offset + band_row_span,
                    column_offset : column_offset + column_count,
                ]
            )
            v_local = (
                v_local
                + local_kernel_weight[row_offset, column_offset]
                * gpad[
                    2 - row_offset : 2 - row_offset + band_row_span,
                    2 - column_offset : 2 - column_offset + column_count,
                ]
            )
            kernel_row_slice.append(
                jnp.sum(
                    complete_gradient
                    * value_padded[
                        row_offset : row_offset + band_row_span,
                        column_offset : column_offset + column_count,
                    ],
                    axis=(0, 1),
                )
            )
    mixed_out = (attn.reshape(band_row_span, column_count, width) + local_output).astype(
        jnp.bfloat16
    )[None]
    grad_flat = complete_gradient.reshape(count, width)
    scaled = grad_flat / den_wide
    den_grad = -jnp.dot(grad_flat * attn, indicator, precision=high) / den
    den_grad_wide = jnp.dot(den_grad, indicator.T, precision=high)
    back_state = block_outer(q_wide, scaled, group_count, group_heads, True)
    back_norm = jnp.sum(q_wide * den_grad_wide, axis=0).reshape(HEADS, HEAD_DIM)
    later_state, later_norm = frame_totals((back_state, back_norm), True)
    query_grad = apply_blocks(scaled, state_blocks, True) + den_grad_wide * norm_flat
    query_grad = (
        (query_grad * slope(q_raw))
        .reshape(band_row_span, column_count, width)
        .astype(jnp.bfloat16)[None]
    )
    later_blocks = block_matrix(later_state, group_count, group_heads)
    key_grad = apply_blocks(
        value_flat.astype(jnp.float32), later_blocks, True
    ) + later_norm.reshape(width)
    key_grad = (
        (key_grad * slope(k_raw))
        .reshape(band_row_span, column_count, width)
        .astype(jnp.bfloat16)[None]
    )
    value_grad = apply_blocks(k_feat.astype(jnp.float32), later_blocks, False)
    value_grad = (value_grad.reshape(band_row_span, column_count, width) + v_local).astype(
        jnp.bfloat16
    )[None]
    kernel_terms = jnp.stack(kernel_row_slice).reshape(3, 3, width)
    kernel_total = lax.psum(kernel_terms, ("tm", "band"))
    total_tokens = lax.axis_size("tm") * lax.axis_size("band") * count
    kernel_grad = kernel_total / math.sqrt(total_tokens)
    return (mixed_out, query_grad, key_grad, value_grad, kernel_grad)


def solution(mesh):
    placed = (
        P("tm", "band", None, None),
        P("tm", "band", None, None),
        P("tm", "band", None, None),
        P("tm", "band", None, None),
        P(),
    )
    return jax.shard_map(
        shards,
        mesh=mesh,
        in_specs=placed,
        out_specs=(
            P("tm", "band", None, None),
            P("tm", "band", None, None),
            P("tm", "band", None, None),
            P("tm", "band", None, None),
            P(),
        ),
        check_vma=False,
    )
```

profile of v0, /device:TPU:1, one launch (start us, length us, event | category | flops | bytes accessed | tf_op | source)
XLA Modules:
  0.0 863.7 jit_solution(13523367854085724787)
XLA Ops:
  10.0 2.6 reshape.180
  12.5 4.8 multiply_reduce_fusion.1
  17.4 79.9 %all-reduce.4.cloned.1.call-done = f32[35,32,32]{2,1,0:T(8,128)} async-done(((f32[35,32,32]{2,1,0:T(8,128)}), f32[35,32,32]{2,1,0:T(8,128)}) %all-reduce.4.cloned.1.call-update) | async-done | bytes 143376 | tf_op jit(solution)/shard_map/psum | solution.py:59
  97.5 22.3 %psum.36 = f32[35,32]{1,0:T(8,128)S(1)} all-reduce(f32[35,32]{1,0:T(8,128)S(1)} %reshape.182), channel_id=1, replica_groups=mesh['tm'=64,'band'=8] {'band'}, use_global_device_ids=true, to_apply=%region_3.4 | all-reduce | flops 1120 | bytes 8960 | tf_op jit(solution)/shard_map/psum | solution.py:59
  121.4 1.3 select_n.138
  123.8 69.4 %all-gather.4 = f32[64,35,32]{1,2,0:T(8,128)} all-gather(f32[1,35,32]{1,2,0:T(8,128)S(1)} %copy.44), channel_id=3, replica_groups=mesh['tm'=64,'band'=8] {'tm'}, dimensions={0}, use_global_device_ids=true | all-gather | bytes 291200 | tf_op jit(solution)/shard_map/all_gather | solution.py:13
  193.2 69.6 %all-gather.9.cloned.1.call-done = f32[2240,32,32]{2,1,0:T(8,128)} async-done(((f32[35,32,32]{2,1,0:T(8,128)}), f32[2240,32,32]{2,1,0:T(8,128)}) %all-gather.9.cloned.1.call-update) | async-done | bytes 9175056 | tf_op jit(solution)/shard_map/all_gather | solution.py:13
  262.8 135.1 %while.34 = (s32[]{:T(128)}, f32[35,32,32]{2,1,0:T(8,128)S(1)}, f32[35,32]{1,0:T(8,128)S(1)}, s32[]{:T(128)}, f32[64,35,32,32]{3,2,1,0:T(8,128)}, /*index=5*/f32[64,35,32]{1,2,0:T(8,128)}, s32[]{:T(128)}, s32[]{:T(128)}) while((s32[]{:T(128)}, f32[35,32,32]{2,1,0:T(8,128)S(1)}, f32[35,32]{1,0:T(8,128)S(1)}, s32[]{:T(128)}, ...), condition=%wide.region_5.6_spmd.clone, body=%wide.region_4.5_spmd.clone.sunk | while | flops 110884 | bytes 461555 | solution.py:26
  262.8 1.3 add_select_fusion.9
  264.9 1.3 add_select_fusion.9
  267.1 1.3 add_select_fusion.9
  269.2 1.3 add_select_fusion.9
  271.3 1.3 add_select_fusion.9
  273.4 1.3 add_select_fusion.9
  275.5 1.3 add_select_fusion.9
  277.6 1.3 add_select_fusion.9
  279.7 1.3 add_select_fusion.9
  281.8 1.3 add_select_fusion.9
  283.9 1.3 add_select_fusion.9
  286.0 1.3 add_select_fusion.9
  288.1 1.3 add_select_fusion.9
  398.0 2.4 mul.264
  400.4 3.6 mul.265
  405.9 2.4 reshape.183
  409.2 3.0 fusion.73
  412.2 1.5 reshape.185
  413.7 2.0 fusion.49
  415.7 3.9 reshape.187
  419.6 4.8 multiply_reduce_fusion
  424.4 70.0 %all-reduce.6.cloned.1.call-done = f32[35,32,32]{2,1,0:T(8,128)} async-done(((f32[35,32,32]{2,1,0:T(8,128)}), f32[35,32,32]{2,1,0:T(8,128)}) %all-reduce.6.cloned.1.call-update) | async-done | bytes 143376 | tf_op jit(solution)/shard_map/psum | solution.py:59
  494.6 3.2 collective-permute-start
  497.8 1.5 collective-permute-start.1
  499.3 2.0 select_n.142
  501.4 2.2 collective-permute-done.1
  503.6 1.5 fusion.10
  506.2 107.4 %psum.39 = f32[3,3,1120]{2,1,0:T(4,128)S(1)} all-reduce(f32[3,3,1120]{2,1,0:T(4,128)S(1)} %reshape.191), channel_id=1, replica_groups=mesh['tm'=64,'band'=8] {'tm','band'}, use_global_device_ids=true, to_apply=%region_21.22 | all-reduce | flops 10080 | bytes 80640 | tf_op jit(solution)/shard_map/psum | solution.py:204
  614.3 3.1 convolution_bitcast_fusion.3
  618.8 2.1 reshape.184
  620.9 2.2 fusion.4
  624.0 24.1 %psum.38 = f32[35,32]{1,0:T(8,128)S(1)} all-reduce(f32[35,32]{1,0:T(8,128)S(1)} %reshape.189), channel_id=1, replica_groups=mesh['tm'=64,'band'=8] {'band'}, use_global_device_ids=true, to_apply=%region_9.10 | all-reduce | flops 1120 | bytes 8960 | tf_op jit(solution)/shard_map/psum | solution.py:59
  649.0 58.1 %all-gather.5 = f32[64,35,32]{1,2,0:T(8,128)} all-gather(f32[1,35,32]{1,2,0:T(8,128)S(1)} %copy.52), channel_id=5, replica_groups=mesh['tm'=64,'band'=8] {'tm'}, dimensions={0}, use_global_device_ids=true | all-gather | bytes 291200 | tf_op jit(solution)/shard_map/all_gather | solution.py:13
  707.0 1.4 fusion.52
  708.4 135.5 %while.35 = (s32[]{:T(128)}, f32[35,32,32]{2,1,0:T(8,128)S(1)}, f32[35,32]{1,0:T(8,128)S(1)}, s32[]{:T(128)}, f32[64,35,32,32]{3,2,1,0:T(8,128)}, /*index=5*/f32...) while((s32[]{:T(128)}, f32[35,32,32]{2,1,0:T(8,128)S(1)}, ...), condition=%wide.region_11.12_spmd.clone, body=%wide.region_10.11_spmd.clone.sunk | while | flops 110888 | bytes 461617 | solution.py:26
  708.4 1.3 add_select_fusion.11
  844.0 2.4 mul.306
  846.4 3.6 mul.307
  851.1 1.8 convolution_bitcast_fusion.1
  854.8 1.4 fusion.53
  (608 shorter events, 267.0 us)
Async XLA Ops:
  7.2 1.8 copy-start.17
  7.2 90.1 %all-reduce.4.cloned.1.call-start = ((), (), s32[]{:S(2)}) async-start(), calls=%async_computation | async-start | bytes 1146880 | tf_op jit(solution)/shard_map/psum | solution.py:59
  9.0 1.0 copy-start.5
  9.5 3.0 copy-start.7
  17.4 245.4 %all-gather.9.cloned.1.call-start = ((), (), s32[]{:S(2)}) async-start(), calls=%async_computation.2 | async-start | bytes 37273600 | tf_op jit(solution)/shard_map/all_gather | solution.py:13
  97.3 22.9 %copy-start.20 = (bf16[1,5,26,1120]{3,2,1,0:T(8,128)(2,1)S(1)}, bf16[1,5,26,1120]{3,2,1,0:T(8,128)(2,1)}, u32[]{:S(2)}) copy-start(bf16[1,5,26,1120]{3,2,1,0:T(8,128)(2,1)} %param.9) | copy-start | bytes 873604
  97.3 397.1 %all-reduce.6.cloned.1.call-start = ((), (), s32[]{:S(2)}) async-start(), calls=%async_computation.1 | async-start | bytes 1146880 | tf_op jit(solution)/shard_map/psum | solution.py:59
  121.4 1.4 copy-start.3
  122.7 285.6 %copy-start.1 = (f32[130,1120]{1,0:T(8,128)}, f32[130,1120]{1,0:T(8,128)S(1)}, u32[]{:S(2)}) copy-start(f32[130,1120]{1,0:T(8,128)S(1)} %reshape.192) | copy-start | bytes 1747204
  262.8 135.1 %copy-start.16 = (f32[35,32,32]{2,1,0:T(8,128)S(1)}, f32[35,32,32]{2,1,0:T(8,128)}, u32[]{:S(2)}) copy-start(f32[35,32,32]{2,1,0:T(8,128)} %all-reduce.4.cloned.1.call-done) | copy-start | bytes 430084
  400.4 3.6 copy-start.9
  412.2 1.5 copy-start.10
  413.7 5.8 copy-start
  424.4 70.1 %copy-start.18 = (bf16[1,5,26,1120]{3,2,1,0:T(8,128)(2,1)S(1)}, bf16[1,5,26,1120]{3,2,1,0:T(8,128)(2,1)}, u32[]{:S(2)}) copy-start(bf16[1,5,26,1120]{3,2,1,0:T(8,128)(2,1)} %param.11) | copy-start | bytes 873604
  424.4 284.0 %all-gather.11.cloned.1.call-start = ((), (), s32[]{:S(2)}) async-start(), calls=%async_computation.3 | async-start | bytes 37273600 | tf_op jit(solution)/shard_map/all_gather | solution.py:13
  494.5 3.2 copy-start.12
  494.5 6.8 copy-start.21
  494.6 6.9 collective-permute-start
  497.8 5.9 collective-permute-start.1
  618.8 4.3 copy-start.2
  620.9 2.2 copy-start.13
  620.9 2.2 copy-start.14
  623.9 83.1 %copy-start.4 = (f32[5,26,1120]{2,1,0:T(8,128)S(1)}, f32[5,26,1120]{2,1,0:T(8,128)}, u32[]{:S(2)}) copy-start(f32[5,26,1120]{2,1,0:T(8,128)} %reshape.184) | copy-start | bytes 1747204
  708.4 135.5 %copy-start.15 = (f32[35,32,32]{2,1,0:T(8,128)S(1)}, f32[35,32,32]{2,1,0:T(8,128)}, u32[]{:S(2)}) copy-start(f32[35,32,32]{2,1,0:T(8,128)} %all-reduce.6.cloned.1.call-done) | copy-start | bytes 430084
  846.4 3.6 copy-start.6
  850.0 1.0 copy-start.8
  853.1 1.1 copy-start.11
  854.8 1.4 copy-start.19
Sparse Core Ops, SparseCore 0:
  17.5 79.7 all-reduce.3
  100.6 162.1 all-gather.8
  424.5 69.8 all-reduce.5
  497.6 161.7 all-gather.10
where the time goes:
time: 877 us; the launch traced here: 864 us
  blocking collectives  281 us (32%)
  waiting for transfers between devices  222 us (25%)
  other arithmetic  182 us (21%)
  local copies, waits for them, and re-layouts  141 us (16%)
  matrix products  15.3 us (2%)
  between operations  14.3 us (2%)
    select_n x256, other arithmetic, step(): return jax.tree.map(lambda a, b: jnp.where(reached, a, b), new, before)  163 us
    psum x2, waiting for transfers between devices, frame_totals(): frame = lax.psum(terms, 'band')  150 us
    all_gather x2, blocking collectives, entering(): everything = jax.tree.map(lambda part: lax.all_gather(part, axis), shard)  127 us
    psum x1, blocking collectives, shards(): kernel_total = lax.psum(kernel_terms, ('tm', 'band'))  107 us
    dynamic_slice x256, local copies, waits for them, and re-layouts, step(): new = combine(before, jax.tree.map(lambda part: part[at], everything))  104 us
    all_gather x2, waiting for transfers between devices, entering(): everything = jax.tree.map(lambda part: lax.all_gather(part, axis), shard)  69.6 us
    psum x2, blocking collectives, frame_totals(): frame = lax.psum(terms, 'band')  46.4 us
  transfers between devices with their start and end apart: 6, of which 4 were waited for; matrix products, arithmetic and copies ran while one was open for 2% of the time, Pallas kernels for 0%

commit v1 on v0

--- a/solution.py
+++ b/solution.py
@@ -201,7 +201,7 @@
         jnp.bfloat16
     )[None]
     kernel_terms = jnp.stack(kernel_row_slice).reshape(3, 3, width)
-    kernel_total = lax.psum(kernel_terms, ("tm", "band"))
+    kernel_total = lax.psum(lax.psum(kernel_terms, "band"), "tm")
     total_tokens = lax.axis_size("tm") * lax.axis_size("band") * count
     kernel_grad = kernel_total / math.sqrt(total_tokens)
     return (mixed_out, query_grad, key_grad, value_grad, kernel_grad)

time: 877 us -> 1030 us (1.17)
  blocking collectives: 281 us -> 432 us
    psum x1, blocking collectives: 107 us -> 255 us  [shards(): kernel_total = lax.psum(lax.psum(kernel_terms, 'band'), 'tm')]
  transfers between devices with their start and end apart: 6 -> 6, of which waited for: 4 -> 3; matrix products, arithmetic and copies ran while one was open for 2% -> 2% of each run, Pallas kernels for 0% -> 0%
where the time goes in v1:
time: 1030 us; the launch traced here: 1020 us
  blocking collectives  432 us (42%)
  waiting for transfers between devices  219 us (21%)
  other arithmetic  181 us (18%)
  local copies, waits for them, and re-layouts  145 us (14%)
  matrix products  15 us (1%)
  between operations  14.3 us (1%)
    psum x1, blocking collectives, shards(): kernel_total = lax.psum(lax.psum(kernel_terms, 'band'), 'tm')  255 us
    select_n x256, other arithmetic, step(): return jax.tree.map(lambda a, b: jnp.where(reached, a, b), new, before)  163 us
    psum x2, waiting for transfers between devices, frame_totals(): frame = lax.psum(terms, 'band')  150 us
    all_gather x2, blocking collectives, entering(): everything = jax.tree.map(lambda part: lax.all_gather(part, axis), shard)  128 us
    dynamic_slice x256, local copies, waits for them, and re-layouts, step(): new = combine(before, jax.tree.map(lambda part: part[at], everything))  104 us
    all_gather x2, waiting for transfers between devices, entering(): everything = jax.tree.map(lambda part: lax.all_gather(part, axis), shard)  69.6 us
    psum x2, blocking collectives, frame_totals(): frame = lax.psum(terms, 'band')  48.4 us
  transfers between devices with their start and end apart: 6, of which 3 were waited for; matrix products, arithmetic and copies ran while one was open for 2% of the time, Pallas kernels for 0%

profile of v1, /device:TPU:1, one launch (start us, length us, event | category | flops | bytes accessed | tf_op | source)
XLA Modules:
  0.0 1015.5 jit_solution(7642302817372191673)
XLA Ops:
  7.2 1.5 reshape_reshape_squeeze.3
  10.0 2.6 reshape.180
  12.5 4.8 multiply_reduce_fusion.1
  17.4 79.9 %all-reduce.5.cloned.1.call-done = f32[35,32,32]{2,1,0:T(8,128)} async-done(((f32[35,32,32]{2,1,0:T(8,128)}), f32[35,32,32]{2,1,0:T(8,128)}) %all-reduce.5.cloned.1.call-update) | async-done | bytes 143376 | tf_op jit(solution)/shard_map/psum | solution.py:59
  98.4 22.5 %psum.43 = f32[35,32]{1,0:T(8,128)S(1)} all-reduce(f32[35,32]{1,0:T(8,128)S(1)} %reshape.182), channel_id=1, replica_groups=mesh['tm'=64,'band'=8] {'band'}, use_global_device_ids=true, to_apply=%region_3.4 | all-reduce | flops 1120 | bytes 8960 | tf_op jit(solution)/shard_map/psum | solution.py:59
  122.4 1.3 select_n.138
  123.8 69.4 %all-gather.4 = f32[64,35,32]{1,2,0:T(8,128)} all-gather(f32[1,35,32]{1,2,0:T(8,128)S(1)} %copy.44), channel_id=3, replica_groups=mesh['tm'=64,'band'=8] {'tm'}, dimensions={0}, use_global_device_ids=true | all-gather | bytes 291200 | tf_op jit(solution)/shard_map/all_gather | solution.py:13
  193.2 69.6 %all-gather.9.cloned.1.call-done = f32[2240,32,32]{2,1,0:T(8,128)} async-done(((f32[35,32,32]{2,1,0:T(8,128)}), f32[2240,32,32]{2,1,0:T(8,128)}) %all-gather.9.cloned.1.call-update) | async-done | bytes 9175056 | tf_op jit(solution)/shard_map/all_gather | solution.py:13
  262.7 135.1 %while.34 = (s32[]{:T(128)}, f32[35,32,32]{2,1,0:T(8,128)S(1)}, f32[35,32]{1,0:T(8,128)S(1)}, s32[]{:T(128)}, f32[64,35,32,32]{3,2,1,0:T(8,128)}, /*index=5*/f32[64,35,32]{1,2,0:T(8,128)}, s32[]{:T(128)}, s32[]{:T(128)}) while((s32[]{:T(128)}, f32[35,32,32]{2,1,0:T(8,128)S(1)}, f32[35,32]{1,0:T(8,128)S(1)}, s32[]{:T(128)}, ...), condition=%wide.region_5.6_spmd.clone, body=%wide.region_4.5_spmd.clone.sunk | while | flops 110884 | bytes 461563 | solution.py:26
  262.7 1.3 add_select_fusion.9
  264.9 1.3 add_select_fusion.9
  267.0 1.3 add_select_fusion.9
  269.1 1.3 add_select_fusion.9
  271.2 1.3 add_select_fusion.9
  273.4 1.3 add_select_fusion.9
  275.5 1.3 add_select_fusion.9
  277.6 1.3 add_select_fusion.9
  279.7 1.3 add_select_fusion.9
  281.8 1.3 add_select_fusion.9
  283.9 1.3 add_select_fusion.9
  397.9 2.4 mul.264
  400.3 3.6 mul.265
  405.8 2.4 reshape.183
  409.1 3.0 fusion.73
  412.2 1.5 reshape.185
  413.7 2.0 fusion.49
  415.7 3.9 reshape.187
  419.5 4.8 multiply_reduce_fusion
  424.4 70.0 %all-reduce.7.cloned.1.call-done = f32[35,32,32]{2,1,0:T(8,128)} async-done(((f32[35,32,32]{2,1,0:T(8,128)}), f32[35,32,32]{2,1,0:T(8,128)}) %all-reduce.7.cloned.1.call-update) | async-done | bytes 143376 | tf_op jit(solution)/shard_map/psum | solution.py:59
  495.4 1.3 collective-permute-start.1
  496.7 4.2 collective-permute-start
  501.0 2.0 select_n.142
  503.1 1.5 fusion.10
  505.7 2.0 reshape.184
  507.7 2.8 convolution_bitcast_fusion.3
  510.5 1.3 copy.49
  511.8 2.5 reshape.186
  514.3 2.2 fusion.4
  518.2 26.0 %all-reduce.1 = (f32[35,32]{1,0:T(8,128)S(1)}, f32[3,3,1120]{2,1,0:T(4,128)S(1)}) all-reduce(f32[35,32]{1,0:T(8,128)S(1)} %reshape.189, f32[3,3,1120]{2,1,0:T(4,128)S(1)} %reshape.191), channel_id=1, replica_groups=mesh['tm'=64,'band'=8] {'band'}, use_global_device_ids=true, to_apply=%region_9.10 | all-reduce | flops 11200 | bytes 89600 | tf_op jit(solution)/shard_map/psum | solution.py:59
  544.2 255.4 %psum.47 = f32[3,3,1120]{2,1,0:T(4,128)S(1)} all-reduce(f32[3,3,1120]{2,1,0:T(4,128)S(1)} %get-tuple-element.371), channel_id=1, replica_groups=mesh['tm'=64,'band'=8] {'tm'}, use_global_device_ids=true, to_apply=%region_22.23 | all-reduce | flops 10080 | bytes 80640 | tf_op jit(solution)/shard_map/psum | solution.py:204
  799.6 58.4 %all-gather.5 = f32[64,35,32]{1,2,0:T(8,128)} all-gather(f32[1,35,32]{1,2,0:T(8,128)S(1)} %copy.52), channel_id=5, replica_groups=mesh['tm'=64,'band'=8] {'tm'}, dimensions={0}, use_global_device_ids=true | all-gather | bytes 291200 | tf_op jit(solution)/shard_map/all_gather | solution.py:13
  858.6 1.4 fusion.52
  860.0 135.4 %while.35 = (s32[]{:T(128)}, f32[35,32,32]{2,1,0:T(8,128)S(1)}, f32[35,32]{1,0:T(8,128)S(1)}, s32[]{:T(128)}, f32[64,35,32,32]{3,2,1,0:T(8,128)}, /*index=5*/f32...) while((s32[]{:T(128)}, f32[35,32,32]{2,1,0:T(8,128)S(1)}, ...), condition=%wide.region_11.12_spmd.clone, body=%wide.region_10.11_spmd.clone.sunk | while | flops 110888 | bytes 461625 | solution.py:26
  860.0 1.3 add_select_fusion.11
  995.5 2.4 mul.306
  997.9 3.6 mul.307
  1002.5 1.5 convolution_bitcast_fusion
  1007.6 1.4 fusion.53
  (608 shorter events, 267.9 us)
Async XLA Ops:
  7.2 1.6 copy-start.18
  7.2 90.1 %all-reduce.5.cloned.1.call-start = ((), (), s32[]{:S(2)}) async-start(), calls=%async_computation | async-start | bytes 1146880 | tf_op jit(solution)/shard_map/psum | solution.py:59
  8.7 1.2 copy-start.5
  9.5 3.0 copy-start.7
  17.3 80.1 %copy-start.3 = (bf16[1,5,26,1120]{3,2,1,0:T(8,128)(2,1)S(1)}, bf16[1,5,26,1120]{3,2,1,0:T(8,128)(2,1)}, u32[]{:S(2)}) copy-start(bf16[1,5,26,1120]{3,2,1,0:T(8,128)(2,1)} %param.12) | copy-start | bytes 873604
  17.3 245.4 %all-gather.9.cloned.1.call-start = ((), (), s32[]{:S(2)}) async-start(), calls=%async_computation.2 | async-start | bytes 37273600 | tf_op jit(solution)/shard_map/all_gather | solution.py:13
  97.3 397.1 %all-reduce.7.cloned.1.call-start = ((), (), s32[]{:S(2)}) async-start(), calls=%async_computation.1 | async-start | bytes 1146880 | tf_op jit(solution)/shard_map/psum | solution.py:59
  98.3 23.0 %copy-start.20 = (bf16[1,5,26,1120]{3,2,1,0:T(8,128)(2,1)S(1)}, bf16[1,5,26,1120]{3,2,1,0:T(8,128)(2,1)}, u32[]{:S(2)}) copy-start(bf16[1,5,26,1120]{3,2,1,0:T(8,128)(2,1)} %param.9) | copy-start | bytes 873604
  123.7 284.6 %copy-start.1 = (f32[130,1120]{1,0:T(8,128)}, f32[130,1120]{1,0:T(8,128)S(1)}, u32[]{:S(2)}) copy-start(f32[130,1120]{1,0:T(8,128)S(1)} %reshape.192) | copy-start | bytes 1747204
  262.7 135.1 %copy-start.16 = (f32[35,32,32]{2,1,0:T(8,128)S(1)}, f32[35,32,32]{2,1,0:T(8,128)}, u32[]{:S(2)}) copy-start(f32[35,32,32]{2,1,0:T(8,128)} %all-reduce.5.cloned.1.call-done) | copy-start | bytes 430084
  400.3 3.6 copy-start.9
  412.2 1.5 copy-start.10
  413.7 5.8 copy-start
  424.3 70.1 %copy-start.17 = (bf16[1,5,26,1120]{3,2,1,0:T(8,128)(2,1)S(1)}, bf16[1,5,26,1120]{3,2,1,0:T(8,128)(2,1)}, u32[]{:S(2)}) copy-start(bf16[1,5,26,1120]{3,2,1,0:T(8,128)(2,1)} %param.11) | copy-start | bytes 873604
  424.4 435.6 %all-gather.11.cloned.1.call-start = ((), (), s32[]{:S(2)}) async-start(), calls=%async_computation.3 | async-start | bytes 37273600 | tf_op jit(solution)/shard_map/all_gather | solution.py:13
  494.5 0.9 copy-start.12
  495.4 7.6 copy-start.21
  495.4 7.7 collective-permute-start.1
  496.7 6.4 collective-permute-start
  511.8 4.6 copy-start.2
  514.3 2.2 copy-start.13
  514.3 2.2 copy-start.14
  517.2 341.4 %copy-start.4 = (f32[5,26,1120]{2,1,0:T(8,128)S(1)}, f32[5,26,1120]{2,1,0:T(8,128)}, u32[]{:S(2)}) copy-start(f32[5,26,1120]{2,1,0:T(8,128)} %reshape.184) | copy-start | bytes 1747204
  860.0 135.4 %copy-start.15 = (f32[35,32,32]{2,1,0:T(8,128)S(1)}, f32[35,32,32]{2,1,0:T(8,128)}, u32[]{:S(2)}) copy-start(f32[35,32,32]{2,1,0:T(8,128)} %all-reduce.7.cloned.1.call-done) | copy-start | bytes 430084
  997.9 3.6 copy-start.6
  1001.5 1.0 copy-start.8
  1004.3 1.1 copy-start.11
  1005.7 1.0 copy-start.19
Sparse Core Ops, SparseCore 0:
  17.5 79.7 all-reduce.4
  100.6 162.1 all-gather.8
  424.5 69.8 all-reduce.6
  497.5 161.2 all-gather.10
